TPU v7x, 32 devices: a whole 2x2x4 slice. The times are simulated.
32 devices in a mesh: head: 8 (over z, y), fsdp: 4 (over x, core).
Axes of the slice: x: 2, y: 2, z: 4, core: 2. Of those that a mesh axis runs over, the one named last changes fastest.
Arguments:
- hidden: bfloat16 [4, 1024, 2048], P('fsdp', 'head'), may hold values from -6 to 6
- w_qkv: bfloat16 [2048, 6144], P(('head', 'fsdp')), may hold values from -0.125 to 0.125
- w_out: bfloat16 [2048, 2048], P(('head', 'fsdp')), may hold values from -0.75 to 0.75
- w_router: bfloat16 [2048, 16], P(('head', 'fsdp')), may hold values from -0.0625 to 0.0625
- g_attn: bfloat16 [2048], P(('head', 'fsdp')), may hold values from 0.099609375 to 1.8984375
- g_ffn: bfloat16 [2048], P(('head', 'fsdp')), may hold values from 0.099609375 to 1.8984375
- g_q: bfloat16 [2048], P(('head', 'fsdp')), may hold values from 0.69921875 to 2
- g_k: bfloat16 [2048], P(('head', 'fsdp')), may hold values from 0.69921875 to 2
- w_gate: bfloat16 [16, 2048, 1024], P('head', 'fsdp'), may hold values from -0.125 to 0.125
- w_up: bfloat16 [16, 2048, 1024], P('head', 'fsdp'), may hold values from -0.125 to 0.125
- w_down: bfloat16 [16, 1024, 2048], P('head', 'fsdp'), may hold values from -0.75 to 0.75
- lengths: int32 [4], P('fsdp'), may hold values from 256 to 1024, as said below
- routes: int32 [4, 1024, 8], P('fsdp', 'head'), may hold values from 0 to 15, all different within a row; in each aligned block of 128 rows (0 to 127, 128 to 255, ..., all dimensions but the last counted through in order) at most 96 rows name the same one
- route_codes: int32 [4, 1024, 8], P('fsdp', 'head'), may hold values from -384 to 383
- cotangent: bfloat16 [4, 1024, 2048], P('fsdp', 'head'), may hold values from -6 to 6
Outputs:
- out: bfloat16 [4, 1024, 2048], P('fsdp', 'head')
- d_hidden: float32 [4, 1024, 2048], P('fsdp', 'head')
- d_w_qkv: float32 [2048, 6144], P(('head', 'fsdp'))
- d_w_out: float32 [2048, 2048], P(('head', 'fsdp'))
- d_w_router: float32 [2048, 16], P(('head', 'fsdp'))
- d_g_attn: float32 [2048], P(('head', 'fsdp'))
- d_g_ffn: float32 [2048], P(('head', 'fsdp'))
- d_g_q: float32 [2048], P(('head', 'fsdp'))
- d_g_k: float32 [2048], P(('head', 'fsdp'))
- d_w_gate: float32 [16, 2048, 1024], P('head', 'fsdp')
- d_w_up: float32 [16, 2048, 1024], P('head', 'fsdp')
- d_w_down: float32 [16, 1024, 2048], P('head', 'fsdp')
Inputs may be any that keep to these rules, and one draw needn't show every extreme that they name: `lengths`: keys at positions at or after a sequence's length are masked. Some sequence has 1024 valid slots, some 1024 // 4. Each token names 8 different experts. In the 128 tokens of one device no expert is named by more than 96 routes, and some expert reaches 96.
All inputs are finite; a program needn't handle non-finite values.
Results may differ from a plain program's by a relative error of at most 0.018.
Values may be sent and summed in bfloat16 or wider, within the bound.
A program may use at most 256 MiB of HBM per device.

v0:
```python
import math
import jax
import jax.numpy as jnp
from jax import lax
from jax.sharding import PartitionSpec as P

HEADS = 16
HD = 128
FF = 1024
TOP = 8
EXP_DEV = 2
EPS = 1e-06
ROPE_BASE = 10000.0
NEGATIVE = -1e30
BF = jnp.bfloat16
F32 = jnp.float32


def ring_head(n, k):
    k %= n
    return 2 * k if k < n // 2 else 2 * n - 1 - 2 * k


def ring_links(n):
    right = [(ring_head(n, k), ring_head(n, k + 1)) for k in range(n)]
    return (right, [(b, a) for a, b in right])


def ring_place():
    n = lax.axis_size("head")
    me = lax.axis_index("head")
    odd = me % 2
    return (1 - odd) * (me // 2) + odd * (n - 1 - me // 2)


def head_at(offset):
    n = lax.axis_size("head")
    k = (ring_place() + offset + n) % n
    down = k // (n // 2)
    return (1 - down) * 2 * k + down * (2 * n - 1 - 2 * k)


def gather_ring(block):
    n = lax.axis_size("head")
    right, left = ring_links(n)
    half = n // 2
    rows = block.shape[0] // 2
    out = jnp.zeros((n,) + block.shape, block.dtype)

    def put(out, piece, offset):
        return lax.dynamic_update_slice_in_dim(out, piece[None], head_at(offset), 0)

    out = put(out, block, 0)
    r = l = block
    for step in range(1, half):
        r = lax.ppermute(r, "head", right)
        l = lax.ppermute(l, "head", left)
        out = put(out, r, -step)
        out = put(out, l, step)
    a = lax.ppermute(r[:rows], "head", right)
    b = lax.ppermute(l[rows:], "head", left)
    return put(out, jnp.concatenate([a, b], 0), half)


def scatter_ring(parts):
    n = lax.axis_size("head")
    right, left = ring_links(n)
    half = n // 2
    rows = parts.shape[1] // 2

    def piece(offset):
        return lax.dynamic_index_in_dim(parts, head_at(offset), 0, keepdims=False)

    far = piece(half)
    r = lax.ppermute(far[:rows], "head", right)
    l = lax.ppermute(far[rows:], "head", left)
    for step in range(half - 1, 0, -1):
        br = piece(step).astype(F32)
        bl = piece(-step).astype(F32)
        if step == half - 1:
            br = jnp.concatenate([br[:rows] + r.astype(F32), br[rows:]], 0)
            bl = jnp.concatenate([bl[:rows], bl[rows:] + l.astype(F32)], 0)
        else:
            br = br + r.astype(F32)
            bl = bl + l.astype(F32)
        r = lax.ppermute(br.astype(BF), "head", right)
        l = lax.ppermute(bl.astype(BF), "head", left)
    return piece(0).astype(F32) + r.astype(F32) + l.astype(F32)


def rotate(values, cosine, sine):
    half = HD // 2
    shaped = values.reshape(values.shape[0], -1, HD)
    first = shaped[..., :half]
    second = shaped[..., half:]
    turned = jnp.concatenate(
        [first * cosine - second * sine, second * cosine + first * sine], axis=-1
    )
    return turned.reshape(values.shape)


def dot(a, b, dims=((1,), (0,))):
    return lax.dot_general(a, b, (dims, ((), ())), preferred_element_type=F32)


NT = ((1,), (1,))
TN = ((0,), (0,))


def body(
    hidden,
    w_qkv,
    w_out,
    w_router,
    g_attn,
    g_ffn,
    g_q,
    g_k,
    w_gate,
    w_up,
    w_down,
    lengths,
    routes,
    route_codes,
    cotangent,
):
    n = lax.axis_size("head")
    m = lax.axis_size("fsdp")
    me = lax.axis_index("head")
    rows = hidden.shape[1]
    width = hidden.shape[2]
    seq = rows * n
    lh = HEADS // n
    dh = lh * HD
    experts = EXP_DEV * n
    shard = w_qkv.shape[0]
    scale = 1.0 / math.sqrt(HD)
    both = ("head", "fsdp")
    small = jnp.concatenate(
        [w_router, g_attn[:, None], g_ffn[:, None], g_q[:, None], g_k[:, None]], axis=1
    )
    small = lax.all_gather(small, both, axis=0, tiled=True)
    router = small[:, :experts]
    gain_attn = small[:, experts].astype(F32)
    gain_ffn = small[:, experts + 1].astype(F32)
    gains_q = lax.dynamic_slice_in_dim(small[:, experts + 2], me * dh, dh, 0).astype(F32)
    gains_k = lax.dynamic_slice_in_dim(small[:, experts + 3], me * dh, dh, 0).astype(F32)
    cols = w_qkv.reshape(shard, 3, n, dh).transpose(2, 0, 1, 3).reshape(n, shard, 3 * dh)
    cols = lax.all_to_all(cols, "head", split_axis=0, concat_axis=0, tiled=True)
    qkv = lax.all_gather(cols, "fsdp", axis=1, tiled=True).reshape(width, 3 * dh)
    tokens_all = gather_ring(hidden[0]).reshape(seq, width)
    info = gather_ring(jnp.concatenate([routes[0], route_codes[0]], axis=1)).reshape(seq, 2 * TOP)
    full_out = lax.all_gather(w_out, both, axis=0, tiled=True)
    full_gate = lax.all_gather(w_gate, "fsdp", axis=1, tiled=True)
    full_up = lax.all_gather(w_up, "fsdp", axis=1, tiled=True)
    full_down = lax.all_gather(w_down, "fsdp", axis=1, tiled=True)

    def own(values):
        return lax.dynamic_slice_in_dim(values, me * rows, rows, 0)

    def inverse_rms(values):
        return lax.rsqrt(jnp.mean(values * values, axis=-1, keepdims=True) + EPS)

    wide = tokens_all.astype(F32)
    attn_input = (wide * inverse_rms(wide) * gain_attn).astype(BF)
    projected = dot(attn_input, qkv)
    proj_q = projected[:, :dh]
    proj_k = projected[:, dh : 2 * dh]
    squares = jnp.stack([jnp.sum(proj_q * proj_q, axis=1), jnp.sum(proj_k * proj_k, axis=1)])
    squares = lax.psum(squares, "head") / width
    inv_q = lax.rsqrt(squares[0] + EPS)[:, None]
    inv_k = lax.rsqrt(squares[1] + EPS)[:, None]
    frequency = ROPE_BASE ** (-2.0 * jnp.arange(HD // 2, dtype=F32) / HD)
    angles = jnp.arange(seq, dtype=F32)[:, None] * frequency[None, :]
    cosine = jnp.cos(angles)[:, None, :]
    sine = jnp.sin(angles)[:, None, :]
    queries = rotate(proj_q * inv_q * gains_q, cosine, sine).astype(BF)
    keys = rotate(proj_k * inv_k * gains_k, cosine, sine).astype(BF)
    values = projected[:, 2 * dh :].astype(BF)
    valid = jnp.arange(seq, dtype=jnp.int32) < lengths[0]

    def probs_of(q, k):
        scores = jnp.where(valid[None, :], dot(q, k, NT) * scale, NEGATIVE)
        exponent = jnp.exp(scores - jnp.max(scores, axis=-1, keepdims=True))
        return exponent / jnp.sum(exponent, axis=-1, keepdims=True)

    attended = []
    for head in range(lh):
        part = slice(head * HD, (head + 1) * HD)
        probabilities = probs_of(queries[:, part], keys[:, part]).astype(BF)
        attended.append(dot(probabilities, values[:, part]).astype(BF))
    attended = jnp.concatenate(attended, axis=1)
    attended_all = gather_ring(attended).transpose(1, 0, 2).reshape(seq, width)
    residual = wide + dot(attended_all, full_out)
    inv_ffn = inverse_rms(residual)
    ffn_input = (residual * inv_ffn * gain_ffn).astype(BF)
    logits = dot(ffn_input, router)
    matches = info[:, :TOP, None] == jnp.arange(experts, dtype=jnp.int32)[None, None, :]
    chosen = (
        jnp.sum(jnp.where(matches, logits[:, None, :], 0.0), axis=-1)
        + info[:, TOP:].astype(F32) / 1024.0
    )
    chosen = jnp.exp(chosen - jnp.max(chosen, axis=1, keepdims=True))
    gates = chosen / jnp.sum(chosen, axis=1, keepdims=True)
    spread = jnp.sum(jnp.where(matches, gates[:, :, None], 0.0), axis=1)
    mine = lax.dynamic_slice_in_dim(spread, me * EXP_DEV, EXP_DEV, 1)
    cot_all = gather_ring(cotangent[0]).reshape(seq, width)
    mixed = jnp.zeros((seq, width), F32)
    grad_in = jnp.zeros((seq, width), F32)
    gate_dots, gate_grads, up_grads, down_grads = ([], [], [], [])
    for e in range(EXP_DEV):
        gate = mine[:, e : e + 1]
        gate_pre = dot(ffn_input, full_gate[e])
        up_pre = dot(ffn_input, full_up[e])
        sig = jax.nn.sigmoid(gate_pre)
        silu = gate_pre * sig
        act = (silu * up_pre).astype(BF)
        produced = dot(act, full_down[e]).astype(BF).astype(F32)
        mixed = mixed + gate * produced
        cot_f = cot_all.astype(F32)
        gate_dots.append(jnp.sum(produced * cot_f, axis=1))
        grad_out = (gate * cot_f).astype(BF)
        grad_act = dot(grad_out, full_down[e], NT)
        grad_gate_pre = (grad_act * up_pre * sig * (1.0 + gate_pre * (1.0 - sig))).astype(BF)
        grad_up_pre = (grad_act * silu).astype(BF)
        down_grads.append(dot(act, grad_out, TN).astype(BF))
        gate_grads.append(dot(ffn_input, grad_gate_pre, TN).astype(BF))
        up_grads.append(dot(ffn_input, grad_up_pre, TN).astype(BF))
        grad_in = grad_in + dot(grad_gate_pre, full_gate[e], NT) + dot(grad_up_pre, full_up[e], NT)
    grad_ffn = scatter_ring(grad_in.astype(BF).reshape(n, rows, width))
    summed = scatter_ring(mixed.astype(BF).reshape(n, rows, width))

    def over_fsdp(grads):
        return lax.psum_scatter(jnp.stack(grads), "fsdp", scatter_dimension=1, tiled=True).astype(
            F32
        )

    grad_w_gate = over_fsdp(gate_grads)
    grad_w_up = over_fsdp(up_grads)
    grad_w_down = over_fsdp(down_grads)
    dots = jnp.stack(gate_dots).reshape(EXP_DEV, n, rows).transpose(1, 0, 2)
    dots = lax.all_to_all(dots, "head", split_axis=0, concat_axis=0, tiled=True)
    dots = dots.reshape(experts, rows).T
    own_spread = own(spread)
    own_residual = own(residual)
    out_rows = own_residual + summed
    grad_rows = cotangent[0].astype(F32)
    grad_logits = own_spread * (dots - jnp.sum(own_spread * dots, axis=1, keepdims=True))
    high = lax.Precision.HIGHEST
    grad_ffn = grad_ffn + jnp.dot(grad_logits, router.astype(F32).T, precision=high)
    grad_router = jnp.dot(own(ffn_input).astype(F32).T, grad_logits, precision=high)

    def norm_back(values, gain, grad):
        inv = inverse_rms(values)
        unit = values * inv
        scaled = grad * gain
        back = inv * (scaled - unit * jnp.mean(scaled * unit, axis=-1, keepdims=True))
        return (back, jnp.sum(grad * unit, axis=0))

    back, grad_gain_ffn = norm_back(own_residual, gain_ffn, grad_ffn)
    grad_residual = grad_rows + back
    grad_attn_out = grad_residual.astype(BF)
    grad_attended = dot(grad_attn_out, full_out, NT).astype(BF)
    grad_heads = lax.all_to_all(
        grad_attended.reshape(rows, n, dh), "head", split_axis=1, concat_axis=0, tiled=True
    ).reshape(seq, dh)
    grad_q, grad_k, grad_v = ([], [], [])
    for head in range(lh):
        part = slice(head * HD, (head + 1) * HD)
        probabilities = probs_of(queries[:, part], keys[:, part])
        grad_probs = dot(grad_heads[:, part], values[:, part], NT)
        inner = jnp.sum(probabilities * grad_probs, axis=-1, keepdims=True)
        grad_scores = (probabilities * (grad_probs - inner)).astype(BF)
        grad_q.append((dot(grad_scores, keys[:, part]) * scale).astype(BF))
        grad_k.append((dot(grad_scores, queries[:, part], TN) * scale).astype(BF))
        grad_v.append(dot(probabilities.astype(BF), grad_heads[:, part], TN).astype(BF))
    turned_q = rotate(jnp.concatenate(grad_q, axis=1).astype(F32), cosine, -sine)
    turned_k = rotate(jnp.concatenate(grad_k, axis=1).astype(F32), cosine, -sine)
    unit_q = proj_q * inv_q
    unit_k = proj_k * inv_k
    means = jnp.stack(
        [jnp.sum(turned_q * gains_q * unit_q, axis=1), jnp.sum(turned_k * gains_k * unit_k, axis=1)]
    )
    means = lax.psum(means, "head") / width
    grad_projected = jnp.concatenate(
        [
            (inv_q * (turned_q * gains_q - unit_q * means[0][:, None])).astype(BF),
            (inv_k * (turned_k * gains_k - unit_k * means[1][:, None])).astype(BF),
            jnp.concatenate(grad_v, axis=1),
        ],
        axis=1,
    )
    grad_gain_q = jnp.sum(turned_q * unit_q, axis=0)
    grad_gain_k = jnp.sum(turned_k * unit_k, axis=0)
    grad_attn_in = dot(grad_projected, qkv, NT).astype(BF)
    grad_attn_in = scatter_ring(grad_attn_in.reshape(n, rows, width))
    grad_qkv = dot(attn_input, grad_projected, TN).astype(BF).reshape(n, m * shard, 3 * dh)
    grad_qkv = lax.psum_scatter(grad_qkv, "fsdp", scatter_dimension=1, tiled=True)
    grad_qkv = lax.all_to_all(grad_qkv, "head", split_axis=0, concat_axis=0, tiled=True)
    grad_qkv = grad_qkv.reshape(n, shard, 3, dh).transpose(1, 2, 0, 3).reshape(shard, 3 * width)
    grad_all = gather_ring(grad_attn_out).reshape(seq, width)
    grad_out_w = dot(attended, grad_all, TN)
    grad_out_w = lax.psum_scatter(grad_out_w, "fsdp", scatter_dimension=0, tiled=True)
    back, grad_gain_attn = norm_back(hidden[0].astype(F32), gain_attn, grad_attn_in)
    grad_hidden = grad_residual + back

    def at_mine(piece):
        return lax.dynamic_update_slice_in_dim(jnp.zeros((width,), F32), piece, me * dh, 0)[:, None]

    pack = jnp.concatenate(
        [
            grad_router,
            grad_gain_attn[:, None],
            grad_gain_ffn[:, None],
            at_mine(grad_gain_q),
            at_mine(grad_gain_k),
        ],
        axis=1,
    ).reshape(n * m, shard * (experts + 4))
    pack = lax.all_to_all(pack, both, split_axis=0, concat_axis=0, tiled=True)
    pack = jnp.sum(pack, axis=0).reshape(shard, experts + 4)
    return (
        out_rows.astype(BF)[None],
        grad_hidden[None],
        grad_qkv.astype(F32),
        grad_out_w,
        pack[:, :experts],
        pack[:, experts],
        pack[:, experts + 1],
        pack[:, experts + 2],
        pack[:, experts + 3],
        grad_w_gate,
        grad_w_up,
        grad_w_down,
    )


def solution(mesh):
    both = ("head", "fsdp")
    return jax.shard_map(
        body,
        mesh=mesh,
        in_specs=(
            P("fsdp", "head", None),
            P(both, None),
            P(both, None),
            P(both, None),
            P(both),
            P(both),
            P(both),
            P(both),
            P("head", "fsdp", None),
            P("head", "fsdp", None),
            P("head", "fsdp", None),
            P("fsdp"),
            P("fsdp", "head", None),
            P("fsdp", "head", None),
            P("fsdp", "head", None),
        ),
        out_specs=(
            P("fsdp", "head", None),
            P("fsdp", "head", None),
            P(both, None),
            P(both, None),
            P(both, None),
            P(both),
            P(both),
            P(both),
            P(both),
            P("head", "fsdp", None),
            P("head", "fsdp", None),
            P("head", "fsdp", None),
        ),
        check_vma=False,
    )
```

profile of v0, /device:TPU:0, one launch (start us, length us, event | category | flops | bytes accessed | tf_op | source)
XLA Modules:
  0.0 871.2 jit_solution(12422500406623019625)
XLA Ops:
  10.0 27.5 %all_to_all.40 = bf16[8,64,768]{2,1,0:T(8,128)(2,1)} all-to-all(bf16[8,64,768]{2,1,0:T(8,128)(2,1)S(1)} %reshape.375), channel_id=1, replica_groups=mesh['head'=8,'fsdp'=4] {'head'}, dimensions={0} | all-to-all | bytes 1572864 | tf_op jit(solution)/shard_map/all_to_all | solution.py:149
  45.0 53.5 %all-gather = bf16[32,64,20]{1,2,0:T(8,128)(2,1)S(1)} all-gather(bf16[1,64,20]{1,2,0:T(8,128)(2,1)S(1)} %bitcast.496), channel_id=1, replica_groups=mesh['head'=8,'fsdp'=4] {'head','fsdp'}, dimensions={0}, use_global_device_ids=true | all-gather | bytes 84480 | tf_op jit(solution)/shard_map/all_gather | solution.py:142
  127.1 25.3 %collective-permute-done.33 = bf16[128,2048]{1,0:T(8,128)(2,1)} collective-permute-done((bf16[128,2048]{1,0:T(8,128)(2,1)S(1)}, bf16[128,2048]{1,0:T(8,128)(2,1)}, u32[]{:S(2)}, u32[]{:S(2)}) %collective-permute-start.33) | collective-permute-done | bytes 524320 | tf_op jit(solution)/shard_map/ppermute | solution.py:57
  167.3 8.4 collective-permute-done.35
  179.5 7.4 collective-permute-done.5
  190.6 7.6 collective-permute-done.37
  213.6 7.9 fusion.132
  221.7 20.3 %psum.14 = f32[2,1024]{1,0:T(2,128)} all-reduce(f32[2,1024]{1,0:T(2,128)S(1)} %pad_maximum_fusion.17), channel_id=1, replica_groups=mesh['head'=8,'fsdp'=4] {'head'}, use_global_device_ids=true, to_apply=%region_3.4 | all-reduce | flops 2048 | bytes 16384 | tf_op jit(solution)/shard_map/psum | solution.py:170
  258.6 10.1 %collective-permute-done.8 = bf16[1024,256]{0,1:T(8,128)(2,1)S(1)} collective-permute-done((bf16[1024,256]{0,1:T(8,128)(2,1)S(1)}, bf16[1024,256]{0,1:T(8,128)(2,1)S(1)}, u32[]{:S(2)}, u32[]{:S(2)}) %collective-permute-start.8) | collective-permute-done | bytes 524320 | tf_op jit(solution)/shard_map/ppermute | solution.py:56
  302.5 14.3 %multiply_reduce_fusion = (f32[1024]{0:T(1024)S(1)}, f32[1024,2048]{1,0:T(8,128)S(1)}) fusion(bf16[1024,2048]{0,1:T(8,128)(2,1)} %bitcast.38, bf16[2048,2048]{1,0:T(8,128)(2,1)} %all-gather.9.cloned.1.call-done, bf16[8,128,2048]{2,1,0:T(8,128)(2,1)} %fusion.75), kind=kOutput, calls=%fused_computation.30 | convolution fusion | flops 8598322176 | bytes 25169920 | tf_op jit(solution)/shard_map/dot_general | solution.py:103
  329.3 10.0 %fusion.18 = f32[1024,1024]{1,0:T(8,128)} fusion(bf16[1024,2048]{1,0:T(8,128)(2,1)} %copy-done.6, bf16[2,2048,1024]{2,1,0:T(8,128)(2,1)} %all-gather.11.cloned.1.call-done), kind=kOutput, calls=%fused_computation.67 | convolution fusion | flops 4294967296 | bytes 12582912 | tf_op jit(solution)/shard_map/dot_general | solution.py:103
  345.8 10.0 %fusion.20 = f32[1024,1024]{1,0:T(8,128)} fusion(bf16[1024,2048]{1,0:T(8,128)(2,1)} %copy-done.6, bf16[2,2048,1024]{2,1,0:T(8,128)(2,1)} %all-gather.13.cloned.1.call-done), kind=kOutput, calls=%fused_computation.69 | convolution fusion | flops 4294967296 | bytes 12582912 | tf_op jit(solution)/shard_map/dot_general | solution.py:103
  362.0 12.2 %multiply_convert_fusion.5 = (bf16[1024,1024]{1,0:T(8,128)(2,1)S(1)}, bf16[1024,1024]{1,0:T(8,128)(2,1)S(1)}, bf16[1024,1024]{1,0:T(8,128)(2,1)}) fusion(f32[1024,1024]{1,0:T(8,128)} %fusion.18, f32[1024,1024]{1,0:T(8,128)} %fusion.20, bf16[1024,2048]{1,0:T(8,128)(2,1)} %bitcast.454, bf16[2,1024,2048]{2,1,0:T(8,128)(2,1)} %all-gather.15.cloned.1.call-done), kind=kOutput, calls=%fused_computation.49 | convolution fusion | flops 4310695936 | bytes 23068672 | tf_op jit(solution)/shard_map/dot_general | solution.py:103
  374.2 10.4 %fusion.17 = f32[1024,2048]{1,0:T(8,128)} fusion(bf16[1024,1024]{1,0:T(8,128)(2,1)S(1)} %get-tuple-element.89, bf16[2,2048,1024]{2,1,0:T(8,128)(2,1)} %all-gather.11.cloned.1.call-done), kind=kOutput, calls=%fused_computation.66 | convolution fusion | flops 4294967296 | bytes 14680064 | tf_op jit(solution)/shard_map/dot_general | solution.py:103
  384.7 9.1 %fusion.19 = f32[1024,2048]{1,0:T(8,128)} fusion(bf16[1024,1024]{1,0:T(8,128)(2,1)S(1)} %get-tuple-element.88, bf16[2,2048,1024]{2,1,0:T(8,128)(2,1)} %all-gather.13.cloned.1.call-done), kind=kOutput, calls=%fused_computation.68 | convolution fusion | flops 4294967296 | bytes 14680064 | tf_op jit(solution)/shard_map/dot_general | solution.py:103
  393.8 10.4 %multiply_convert_fusion.3 = (bf16[1024,1024]{1,0:T(8,128)(2,1)S(1)}, bf16[1024,1024]{1,0:T(8,128)(2,1)}, bf16[1024,1024]{1,0:T(8,128)(2,1)}) fusion(f32[1024,1024]{1,0:T(8,128)} %fusion.23, f32[1024,1024]{1,0:T(8,128)} %fusion.24, bf16[1024,2048]{1,0:T(8,128)(2,1)S(1)} %bitcast.453, bf16[2,1024,2048]{2,1,0:T(8,128)(2,1)S(1)} %bitcast.530), kind=kOutput, calls=%fused_computation.47 | convolution fusion | flops 4310695936 | bytes 23068672 | tf_op jit(solution)/shard_map/dot_general | solution.py:103
  404.2 9.1 %fusion.22 = f32[1024,2048]{1,0:T(8,128)} fusion(bf16[1024,1024]{1,0:T(8,128)(2,1)} %get-tuple-element.86, bf16[2,2048,1024]{2,1,0:T(8,128)(2,1)S(1)} %bitcast.532), kind=kOutput, calls=%fused_computation.71 | convolution fusion | flops 4294967296 | bytes 14680064 | tf_op jit(solution)/shard_map/dot_general | solution.py:103
  413.4 13.3 %add_convert_fusion = bf16[1024,2048]{1,0:T(8,128)(2,1)} fusion(f32[1024,2048]{1,0:T(8,128)} %fusion.22, f32[1024,2048]{1,0:T(8,128)} %fusion.17, f32[1024,2048]{1,0:T(8,128)} %fusion.19, bf16[1024,1024]{1,0:T(8,128)(2,1)S(1)} %get-tuple-element.85, bf16[2,2048,1024]{2,1,0:T(8,128)(2,1)} %all-gather.13.cloned.1.call-done), kind=kOutput, calls=%fused_computation.28 | convolution fusion | flops 4303355904 | bytes 35651584 | tf_op jit(solution)/shard_map/dot_general | solution.py:103
  440.5 11.3 %collective-permute-done.41 = bf16[128,2048]{1,0:T(8,128)(2,1)S(1)} collective-permute-done((bf16[128,2048]{1,0:T(8,128)(2,1)S(1)}, bf16[128,2048]{1,0:T(8,128)(2,1)S(1)}, u32[]{:S(2)}, u32[]{:S(2)}) %collective-permute-start.41) | collective-permute-done | bytes 524320 | tf_op jit(solution)/shard_map/ppermute | solution.py:86
  453.3 7.5 convolution_convert_fusion.1
  465.8 12.6 %fusion.2 = (f32[1024]{0:T(1024)S(1)}, f32[1024]{0:T(1024)S(1)}, bf16[1024,2048]{1,0:T(8,128)(2,1)}, bf16[1024,2048]{1,0:T(8,128)(2,1)}, bf16[1024,2048]{1,0:T(8,128)(2,1)}) fusion(bf16[8,128,2048]{2,1,0:T(8,128)(2,1)} %fusion.77, bf16[1024,2048]{1,0:T(8,128)(2,1)S(1)} %convolution_convert_fusion.1, f32[1024]{0:T(1024)S(1)} %bitcast.500, ...), kind=kOutput, calls=%fused_computation.6 | convolution fusion | flops 4328519680 | bytes 27279360 | tf_op jit(solution)/shard_map/dot_general | solution.py:103
  542.8 19.8 %psum.15 = f32[2,1024]{1,0:T(2,128)S(1)} all-reduce(f32[2,1024]{1,0:T(2,128)S(1)} %pad_maximum_fusion.18), channel_id=1, replica_groups=mesh['head'=8,'fsdp'=4] {'head'}, use_global_device_ids=true, to_apply=%region_23.24 | all-reduce | flops 2048 | bytes 16384 | tf_op jit(solution)/shard_map/psum | solution.py:284
  570.6 7.6 convert_bitcast_fusion.1
  590.9 7.6 convert_bitcast_fusion.3
  613.1 7.7 convert_bitcast_fusion.5
  647.4 7.6 collective-permute-done.56
  663.5 11.3 %collective-permute-done.58 = bf16[128,2048]{1,0:T(8,128)(2,1)S(1)} collective-permute-done((bf16[128,2048]{1,0:T(8,128)(2,1)S(1)}, bf16[128,2048]{1,0:T(8,128)(2,1)S(1)}, u32[]{:S(2)}, u32[]{:S(2)}) %collective-permute-start.58) | collective-permute-done | bytes 524320 | tf_op jit(solution)/shard_map/ppermute | solution.py:56
  681.4 7.4 collective-permute-done.60
  691.8 8.3 collective-permute-done.49
  762.2 23.2 %collective-permute-done.31 = bf16[128,2048]{1,0:T(8,128)(2,1)S(1)} collective-permute-done((bf16[128,2048]{1,0:T(8,128)(2,1)S(1)}, bf16[128,2048]{1,0:T(8,128)(2,1)S(1)}, u32[]{:S(2)}, u32[]{:S(2)}) %collective-permute-start.31) | collective-permute-done | bytes 524320 | tf_op jit(solution)/shard_map/ppermute | solution.py:87
  802.9 26.6 %reduce-scatter.10.cloned.1.call-done = bf16[2,512,1024]{2,1,0:T(8,128)(2,1)} async-done(((bf16[2,2048,1024]{2,1,0:T(8,128)(2,1)}), bf16[2,512,1024]{2,1,0:T(8,128)(2,1)}) %reduce-scatter.10.cloned.1.call-update) | async-done | bytes 2097168 | tf_op jit(solution)/shard_map/reduce_scatter | solution.py:234
  833.5 30.4 %reduce-scatter.8.cloned.1.call-done = f32[64,2048]{1,0:T(8,128)} async-done(((f32[256,2048]{1,0:T(8,128)}), f32[64,2048]{1,0:T(8,128)}) %reduce-scatter.8.cloned.1.call-update) | async-done | bytes 524304 | tf_op jit(solution)/shard_map/reduce_scatter | solution.py:303
  (527 shorter events, 398.2 us)
Async XLA Ops:
  7.2 206.4 %all-gather.7.cloned.1.call-start = ((), (), s32[]{:S(2)}) async-start(), calls=%async_computation.10 | async-start | bytes 3932160 | tf_op jit(solution)/shard_map/all_gather | solution.py:150
  37.5 265.0 %all-gather.9.cloned.1.call-start = ((), (), s32[]{:S(2)}) async-start(), calls=%async_computation.11 | async-start | bytes 8650752 | tf_op jit(solution)/shard_map/all_gather | solution.py:153
  38.2 291.1 %all-gather.11.cloned.1.call-start = ((), (), s32[]{:S(2)}) async-start(), calls=%async_computation.12 | async-start | bytes 10485760 | tf_op jit(solution)/shard_map/all_gather | solution.py:154
  39.0 306.8 %all-gather.13.cloned.1.call-start = ((), (), s32[]{:S(2)}) async-start(), calls=%async_computation.13 | async-start | bytes 10485760 | tf_op jit(solution)/shard_map/all_gather | solution.py:155
  39.5 322.5 %all-gather.15.cloned.1.call-start = ((), (), s32[]{:S(2)}) async-start(), calls=%async_computation.14 | async-start | bytes 10485760 | tf_op jit(solution)/shard_map/all_gather | solution.py:156
  39.6 69.0 %collective-permute-start.16 = (s32[128,16]{0,1:T(8,128)S(1)}, s32[128,16]{0,1:T(8,128)S(1)}, u32[]{:S(2)}, u32[]{:S(2)}) collective-permute-start(s32[128,16]{0,1:T(8,128)S(1)} %pad_add_fusion), channel_id=1, source_target_pairs={{0,8},{8,16},{16,24},{24,28},{28,20},{20,12},{12,4},{4,0},{1,9},{9... | collective-permute-start | bytes 24584 | tf_op jit(solution)/shard_map/ppermute | solution.py:56
  40.8 67.9 %collective-permute-start.17 = (s32[128,16]{0,1:T(8,128)S(1)}, s32[128,16]{0,1:T(8,128)S(1)}, u32[]{:S(2)}, u32[]{:S(2)}) collective-permute-start(s32[128,16]{0,1:T(8,128)S(1)} %pad_add_fusion), channel_id=1, source_target_pairs={{8,0},{16,8},{24,16},{28,24},{20,28},{12,20},{4,12},{0,4},{9,1},{1... | collective-permute-start | bytes 24584 | tf_op jit(solution)/shard_map/ppermute | solution.py:57
  41.7 80.4 %collective-permute-start = (bf16[128,2048]{1,0:T(8,128)(2,1)S(1)}, bf16[128,2048]{1,0:T(8,128)(2,1)S(1)}, u32[]{:S(2)}, u32[]{:S(2)}) collective-permute-start(bf16[128,2048]{1,0:T(8,128)(2,1)S(1)} %bitcast.420), channel_id=1, source_target_pairs={{0,8},{8,16},{16,24},{24,28},{28,20},{20,12},{12,4},{4,0},{1,9},{9... | collective-permute-start | bytes 1572872 | tf_op jit(solution)/shard_map/ppermute | solution.py:56
  42.8 80.6 %collective-permute-start.1 = (bf16[128,2048]{1,0:T(8,128)(2,1)S(1)}, bf16[128,2048]{1,0:T(8,128)(2,1)S(1)}, u32[]{:S(2)}, u32[]{:S(2)}) collective-permute-start(bf16[128,2048]{1,0:T(8,128)(2,1)S(1)} %bitcast.421), channel_id=1, source_target_pairs={{8,0},{16,8},{24,16},{28,24},{20,28},{12,20},{4,12},{0,4},{9,1},{1... | collective-permute-start | bytes 1572872 | tf_op jit(solution)/shard_map/ppermute | solution.py:57
  43.7 82.2 %collective-permute-start.32 = (bf16[128,2048]{1,0:T(8,128)(2,1)S(1)}, bf16[128,2048]{1,0:T(8,128)(2,1)S(1)}, u32[]{:S(2)}, u32[]{:S(2)}) collective-permute-start(bf16[128,2048]{1,0:T(8,128)(2,1)S(1)} %bitcast.434), channel_id=1, source_target_pairs={{0,8},{8,16},{16,24},{24,28},{28,20},{20,12},{12,4},{4,0},{1,9},{9... | collective-permute-start | bytes 1572872 | tf_op jit(solution)/shard_map/ppermute | solution.py:56
  120.3 32.1 %collective-permute-start.33 = (bf16[128,2048]{1,0:T(8,128)(2,1)S(1)}, bf16[128,2048]{1,0:T(8,128)(2,1)}, u32[]{:S(2)}, u32[]{:S(2)}) collective-permute-start(bf16[128,2048]{1,0:T(8,128)(2,1)S(1)} %bitcast.435), channel_id=1, source_target_pairs={{8,0},{16,8},{24,16},{28,24},{20,28},{12,20},{4,12},{0,4},{9,1},{1... | collective-permute-start | bytes 1572872 | tf_op jit(solution)/shard_map/ppermute | solution.py:57
  122.2 32.2 %collective-permute-start.2 = (bf16[128,2048]{1,0:T(8,128)(2,1)S(1)}, bf16[128,2048]{1,0:T(8,128)(2,1)S(1)}, u32[]{:S(2)}, u32[]{:S(2)}) collective-permute-start(bf16[128,2048]{1,0:T(8,128)(2,1)S(1)} %collective-permute-done), channel_id=1, source_target_pairs={{0,8},{8,16},{16,24},{24,28},{28,20},{20,12},{12,4},{4,0},{1,9},{9... | collective-permute-start | bytes 1572872 | tf_op jit(solution)/shard_map/ppermute | solution.py:56
  123.4 41.0 %collective-permute-start.3 = (bf16[128,2048]{1,0:T(8,128)(2,1)S(1)}, bf16[128,2048]{1,0:T(8,128)(2,1)S(1)}, u32[]{:S(2)}, u32[]{:S(2)}) collective-permute-start(bf16[128,2048]{1,0:T(8,128)(2,1)S(1)} %collective-permute-done.1), channel_id=1, source_target_pairs={{8,0},{16,8},{24,16},{28,24},{20,28},{12,20},{4,12},{0,4},{9,1},{1... | collective-permute-start | bytes 1572872 | tf_op jit(solution)/shard_map/ppermute | solution.py:57
  125.9 38.7 %collective-permute-start.34 = (bf16[128,2048]{1,0:T(8,128)(2,1)S(1)}, bf16[128,2048]{1,0:T(8,128)(2,1)S(1)}, u32[]{:S(2)}, u32[]{:S(2)}) collective-permute-start(bf16[128,2048]{1,0:T(8,128)(2,1)S(1)} %collective-permute-done.32), channel_id=1, source_target_pairs={{0,8},{8,16},{16,24},{24,28},{28,20},{20,12},{12,4},{4,0},{1,9},{9... | collective-permute-start | bytes 1572872 | tf_op jit(solution)/shard_map/ppermute | solution.py:56
  152.4 23.3 %collective-permute-start.35 = (bf16[128,2048]{1,0:T(8,128)(2,1)}, bf16[128,2048]{1,0:T(8,128)(2,1)S(1)}, u32[]{:S(2)}, u32[]{:S(2)}) collective-permute-start(bf16[128,2048]{1,0:T(8,128)(2,1)} %collective-permute-done.33), channel_id=1, source_target_pairs={{8,0},{16,8},{24,16},{28,24},{20,28},{12,20},{4,12},{0,4},{9,1},{1... | collective-permute-start | bytes 1572872 | tf_op jit(solution)/shard_map/ppermute | solution.py:57
  154.3 23.2 %collective-permute-start.4 = (bf16[128,2048]{1,0:T(8,128)(2,1)S(1)}, bf16[128,2048]{1,0:T(8,128)(2,1)S(1)}, u32[]{:S(2)}, u32[]{:S(2)}) collective-permute-start(bf16[128,2048]{1,0:T(8,128)(2,1)S(1)} %collective-permute-done.2), channel_id=1, source_target_pairs={{0,8},{8,16},{16,24},{24,28},{28,20},{20,12},{12,4},{4,0},{1,9},{9... | collective-permute-start | bytes 1572872 | tf_op jit(solution)/shard_map/ppermute | solution.py:56
  164.5 22.5 %collective-permute-start.5 = (bf16[128,2048]{1,0:T(8,128)(2,1)S(1)}, bf16[128,2048]{1,0:T(8,128)(2,1)S(1)}, u32[]{:S(2)}, u32[]{:S(2)}) collective-permute-start(bf16[128,2048]{1,0:T(8,128)(2,1)S(1)} %collective-permute-done.3), channel_id=1, source_target_pairs={{8,0},{16,8},{24,16},{28,24},{20,28},{12,20},{4,12},{0,4},{9,1},{1... | collective-permute-start | bytes 1572872 | tf_op jit(solution)/shard_map/ppermute | solution.py:57
  164.6 22.5 %collective-permute-start.36 = (bf16[128,2048]{1,0:T(8,128)(2,1)S(1)}, bf16[128,2048]{1,0:T(8,128)(2,1)S(1)}, u32[]{:S(2)}, u32[]{:S(2)}) collective-permute-start(bf16[128,2048]{1,0:T(8,128)(2,1)S(1)} %collective-permute-done.34), channel_id=1, source_target_pairs={{0,8},{8,16},{16,24},{24,28},{28,20},{20,12},{12,4},{4,0},{1,9},{9... | collective-permute-start | bytes 1572872 | tf_op jit(solution)/shard_map/ppermute | solution.py:56
  177.6 24.3 %collective-permute-start.6 = (bf16[64,2048]{1,0:T(8,128)(2,1)S(1)}, bf16[64,2048]{1,0:T(8,128)(2,1)S(1)}, u32[]{:S(2)}, u32[]{:S(2)}) collective-permute-start(bf16[64,2048]{1,0:T(8,128)(2,1)S(1)} %slice.410), channel_id=1, source_target_pairs={{0,8},{8,16},{16,24},{24,28},{28,20},{20,12},{12,4},{4,0},{1,9},{9... | collective-permute-start | bytes 786440 | tf_op jit(solution)/shard_map/ppermute | solution.py:60
  188.6 82.4 %collective-permute-start.38 = (bf16[64,2048]{1,0:T(8,128)(2,1)}, bf16[64,2048]{1,0:T(8,128)(2,1)}, u32[]{:S(2)}, u32[]{:S(2)}) collective-permute-start(bf16[64,2048]{1,0:T(8,128)(2,1)} %slice.443), channel_id=1, source_target_pairs={{0,8},{8,16},{16,24},{24,28},{28,20},{20,12},{12,4},{4,0},{1,9},{9... | collective-permute-start | bytes 786440 | tf_op jit(solution)/shard_map/ppermute | solution.py:60
  199.7 71.3 %collective-permute-start.39 = (bf16[64,2048]{1,0:T(8,128)(2,1)}, bf16[64,2048]{1,0:T(8,128)(2,1)}, u32[]{:S(2)}, u32[]{:S(2)}) collective-permute-start(bf16[64,2048]{1,0:T(8,128)(2,1)} %slice.444), channel_id=1, source_target_pairs={{8,0},{16,8},{24,16},{28,24},{20,28},{12,20},{4,12},{0,4},{9,1},{1... | collective-permute-start | bytes 786440 | tf_op jit(solution)/shard_map/ppermute | solution.py:61
  514.4 240.0 %reduce-scatter.6.cloned.1.call-start = ((), (), s32[]{:S(2)}) async-start(), calls=%async_computation.15 | async-start | bytes 3932160 | tf_op jit(solution)/shard_map/reduce_scatter | solution.py:298
  570.4 224.3 %reduce-scatter.14.cloned.1.call-start = ((), (), s32[]{:S(2)}) async-start(), calls=%async_computation.19 | async-start | bytes 10485760 | tf_op jit(solution)/shard_map/reduce_scatter | solution.py:234
  590.8 208.0 %reduce-scatter.12.cloned.1.call-start = ((), (), s32[]{:S(2)}) async-start(), calls=%async_computation.18 | async-start | bytes 10485760 | tf_op jit(solution)/shard_map/reduce_scatter | solution.py:234
  611.2 218.3 %reduce-scatter.10.cloned.1.call-start = ((), (), s32[]{:S(2)}) async-start(), calls=%async_computation.17 | async-start | bytes 10485760 | tf_op jit(solution)/shard_map/reduce_scatter | solution.py:234
  633.2 230.7 %reduce-scatter.8.cloned.1.call-start = ((), (), s32[]{:S(2)}) async-start(), calls=%async_computation.16 | async-start | bytes 2621440 | tf_op jit(solution)/shard_map/reduce_scatter | solution.py:303
  645.2 85.1 %collective-permute-start.29 = (bf16[128,2048]{1,0:T(8,128)(2,1)S(1)}, bf16[128,2048]{1,0:T(8,128)(2,1)}, u32[]{:S(2)}, u32[]{:S(2)}) collective-permute-start(bf16[128,2048]{1,0:T(8,128)(2,1)S(1)} %pad_maximum_fusion.10), channel_id=1, source_target_pairs={{8,0},{16,8},{24,16},{28,24},{20,28},{12,20},{4,12},{0,4},{9,1},{1... | collective-permute-start | bytes 1572872 | tf_op jit(solution)/shard_map/ppermute | solution.py:87
  645.4 74.5 %collective-permute-start.25 = (bf16[128,2048]{1,0:T(8,128)(2,1)S(1)}, bf16[128,2048]{1,0:T(8,128)(2,1)S(1)}, u32[]{:S(2)}, u32[]{:S(2)}) collective-permute-start(bf16[128,2048]{1,0:T(8,128)(2,1)S(1)} %pad_maximum_fusion.9), channel_id=1, source_target_pairs={{0,8},{8,16},{16,24},{24,28},{28,20},{20,12},{12,4},{4,0},{1,9},{9... | collective-permute-start | bytes 1572872 | tf_op jit(solution)/shard_map/ppermute | solution.py:86
  681.3 30.7 %collective-permute-start.53 = (bf16[128,2048]{1,0:T(8,128)(2,1)S(1)}, bf16[128,2048]{1,0:T(8,128)(2,1)}, u32[]{:S(2)}, u32[]{:S(2)}) collective-permute-start(bf16[128,2048]{1,0:T(8,128)(2,1)S(1)} %pad_maximum_fusion.14), channel_id=1, source_target_pairs={{8,0},{16,8},{24,16},{28,24},{20,28},{12,20},{4,12},{0,4},{9,1},{1... | collective-permute-start | bytes 1572872 | tf_op jit(solution)/shard_map/ppermute | solution.py:87
  733.4 24.5 %collective-permute-start.30 = (bf16[128,2048]{1,0:T(8,128)(2,1)}, bf16[128,2048]{1,0:T(8,128)(2,1)}, u32[]{:S(2)}, u32[]{:S(2)}) collective-permute-start(bf16[128,2048]{1,0:T(8,128)(2,1)} %get-tuple-element.113), channel_id=1, source_target_pairs={{8,0},{16,8},{24,16},{28,24},{20,28},{12,20},{4,12},{0,4},{9,1},{1... | collective-permute-start | bytes 1572872 | tf_op jit(solution)/shard_map/ppermute | solution.py:87
  754.4 36.8 %all-to-all-start.3 = ((bf16[8,64,768]{2,1,0:T(8,128)(2,1)}), bf16[8,64,768]{2,1,0:T(8,128)(2,1)S(1)}, u32[]{:S(2)}, u32[]{:S(2)}) async-start(bf16[8,64,768]{2,1,0:T(8,128)(2,1)} %reduce-scatter.6.cloned.1.call-done), calls=%async_computation.4 | async-start | bytes 1572864 | tf_op jit(solution)/shard_map/all_to_all | solution.py:299
  759.3 26.1 %collective-permute-start.31 = (bf16[128,2048]{1,0:T(8,128)(2,1)S(1)}, bf16[128,2048]{1,0:T(8,128)(2,1)S(1)}, u32[]{:S(2)}, u32[]{:S(2)}) collective-permute-start(bf16[128,2048]{1,0:T(8,128)(2,1)S(1)} %fusion.60), channel_id=1, source_target_pairs={{8,0},{16,8},{24,16},{28,24},{20,28},{12,20},{4,12},{0,4},{9,1},{1... | collective-permute-start | bytes 1572872 | tf_op jit(solution)/shard_map/ppermute | solution.py:87
  (141 other events, 2030.4 us)
Sparse Core Ops, SparseCore 0:
  37.6 28.0 all-gather.6
  68.6 92.0 all-gather.8
  162.2 65.0 all-gather.10
  228.8 58.2 all-gather.12
  288.5 58.2 all-gather.14
  570.5 33.8 reduce-scatter.5
  607.1 71.6 reduce-scatter.13
  681.4 73.4 reduce-scatter.11
  757.6 71.7 reduce-scatter.9
  832.4 31.4 reduce-scatter.7
where the time goes:
time: 878 us; the launch traced here: 871 us
  waiting for transfers between devices  278 us (32%)
  matrix products  220 us (25%)
  blocking collectives  121 us (14%)
  other arithmetic  99 us (11%)
  starting transfers between devices  79 us (9%)
  local copies, waits for them, and re-layouts  56.9 us (6%)
  between operations  17.3 us (2%)
    dot_general x37, matrix products, dot(): return lax.dot_general(a, b, (dims, ((), ())), preferred_element_type=F32)  218 us
    ppermute x15, waiting for transfers between devices, gather_ring(): l = lax.ppermute(l, 'head', left)  58.9 us
    all_gather x1, blocking collectives, body(): small = lax.all_gather(small, both, axis=0, tiled=True)  53.5 us
    ppermute x15, waiting for transfers between devices, gather_ring(): r = lax.ppermute(r, 'head', right)  49.1 us
    ppermute x9, waiting for transfers between devices, scatter_ring(): r = lax.ppermute(br.astype(BF), 'head', right)  34.1 us
    ppermute x9, waiting for transfers between devices, scatter_ring(): l = lax.ppermute(bl.astype(BF), 'head', left)  32.8 us
    reduce_scatter x1, waiting for transfers between devices, body(): lax.psum_scatter(grad_out_w, 'fsdp', scatter_dimension=0, tiled=True)  30.4 us
    all_to_all x1, blocking collectives, body(): cols = lax.all_to_all(cols, 'head', split_axis=0, concat_axis=0, tiled=True)  27.5 us
  transfers between devices with their start and end apart: 78, of which 43 were waited for; matrix products, arithmetic and copies ran while one was open for 29% of the time, Pallas kernels for 0%

commit v1 on v0

--- a/solution.py
+++ b/solution.py
@@ -14,6 +14,18 @@
 NEGATIVE = -1e30
 BF = jnp.bfloat16
 F32 = jnp.float32
+
+
+def split_up(shard, dim, size):
+    shape = shard.shape
+    blocks = shard.reshape(*shape[:dim], size, shape[dim] // size, *shape[dim + 1 :])
+    return jnp.moveaxis(blocks, dim, 0)
+
+
+def laid_out(blocks, dim):
+    shape = list(blocks.shape[1:])
+    shape[dim] *= blocks.shape[0]
+    return jnp.moveaxis(blocks, 0, dim).reshape(shape)
 
 
 def ring_head(n, k):
@@ -146,7 +158,14 @@
     gains_q = lax.dynamic_slice_in_dim(small[:, experts + 2], me * dh, dh, 0).astype(F32)
     gains_k = lax.dynamic_slice_in_dim(small[:, experts + 3], me * dh, dh, 0).astype(F32)
     cols = w_qkv.reshape(shard, 3, n, dh).transpose(2, 0, 1, 3).reshape(n, shard, 3 * dh)
-    cols = lax.all_to_all(cols, "head", split_axis=0, concat_axis=0, tiled=True)
+    size, index = (lax.axis_size("head"), lax.axis_index("head"))
+    blocks = split_up(cols, 0, size)
+    outs = [blocks[index]]
+    for lap in range(1, size):
+        sent = blocks[index ^ lap]
+        outs.append(lax.ppermute(sent, "head", [(i, i ^ lap) for i in range(size)]))
+    blocks = jnp.stack(outs)[index ^ jnp.arange(size)]
+    cols = laid_out(blocks, 0)
     qkv = lax.all_gather(cols, "fsdp", axis=1, tiled=True).reshape(width, 3 * dh)
     tokens_all = gather_ring(hidden[0]).reshape(seq, width)
     info = gather_ring(jnp.concatenate([routes[0], route_codes[0]], axis=1)).reshape(seq, 2 * TOP)

time: 878 us -> 879 us (level)
  blocking collectives: 121 us -> 95.6 us
  starting transfers between devices: 79 us -> 92.7 us
  waiting for transfers between devices: 278 us -> 288 us
    all_to_all x1 -> x0, blocking collectives: 27.5 us -> none  [body(): cols = lax.all_to_all(cols, 'head', split_axis=0, concat_axis=0, tiled=True)]
    ppermute x0 -> x7, starting transfers between devices: none -> 12.6 us  [body(): outs.append(lax.ppermute(sent, 'head', [(i, i ^ lap) for i in range(size)]))]
    ppermute x0 -> x7, waiting for transfers between devices: none -> 10.1 us  [body(): outs.append(lax.ppermute(sent, 'head', [(i, i ^ lap) for i in range(size)]))]
    unnamed x195 -> x201, local copies, waits for them, and re-layouts: 18.9 us -> 18.9 us
  transfers between devices with their start and end apart: 78 -> 85, of which waited for: 43 -> 45; matrix products, arithmetic and copies ran while one was open for 29% -> 29% of each run, Pallas kernels for 0% -> 0%
where the time goes in v1:
time: 879 us; the launch traced here: 871 us
  waiting for transfers between devices  288 us (33%)
  matrix products  220 us (25%)
  other arithmetic  99.4 us (11%)
  blocking collectives  95.6 us (11%)
  starting transfers between devices  92.7 us (11%)
  local copies, waits for them, and re-layouts  58.4 us (7%)
  between operations  17.5 us (2%)
    dot_general x37, matrix products, dot(): return lax.dot_general(a, b, (dims, ((), ())), preferred_element_type=F32)  218 us
    ppermute x15, waiting for transfers between devices, gather_ring(): l = lax.ppermute(l, 'head', left)  58 us
    all_gather x1, blocking collectives, body(): small = lax.all_gather(small, both, axis=0, tiled=True)  54.8 us
    ppermute x15, waiting for transfers between devices, gather_ring(): r = lax.ppermute(r, 'head', right)  45 us
    ppermute x9, waiting for transfers between devices, scatter_ring(): r = lax.ppermute(br.astype(BF), 'head', right)  39.6 us
    ppermute x9, waiting for transfers between devices, scatter_ring(): l = lax.ppermute(bl.astype(BF), 'head', left)  33.4 us
    reduce_scatter x1, waiting for transfers between devices, body(): lax.psum_scatter(grad_out_w, 'fsdp', scatter_dimension=0, tiled=True)  30.3 us
    reduce_scatter x3, waiting for transfers between devices, over_fsdp(): lax.psum_scatter(jnp.stack(grads), 'fsdp', scatter_dimension=1, tiled=True)  26.6 us
  transfers between devices with their start and end apart: 85, of which 45 were waited for; matrix products, arithmetic and copies ran while one was open for 29% of the time, Pallas kernels for 0%

profile of v1, /device:TPU:0, one launch (start us, length us, event | category | flops | bytes accessed | tf_op | source)
XLA Modules:
  0.0 871.4 jit_solution(6315554258676717538)
XLA Ops:
  22.8 10.1 %collective-permute-done.12 = bf16[1,64,768]{2,1,0:T(8,128)(2,1)S(1)} collective-permute-done((bf16[1,64,768]{2,1,0:T(8,128)(2,1)S(1)}, bf16[1,64,768]{2,1,0:T(8,128)(2,1)S(1)}, u32[]{:S(2)}, u32[]{:S(2)}) %collective-permute-start.12) | collective-permute-done | bytes 98336 | tf_op jit(solution)/shard_map/ppermute | solution.py:166
  44.9 54.8 %all-gather.1 = bf16[32,64,20]{1,2,0:T(8,128)(2,1)S(1)} all-gather(bf16[1,64,20]{1,2,0:T(8,128)(2,1)S(1)} %bitcast.528), channel_id=1, replica_groups=mesh['head'=8,'fsdp'=4] {'head','fsdp'}, dimensions={0}, use_global_device_ids=true | all-gather | bytes 84480 | tf_op jit(solution)/shard_map/all_gather | solution.py:154
  128.0 24.9 %collective-permute-done.40 = bf16[128,2048]{1,0:T(8,128)(2,1)} collective-permute-done((bf16[128,2048]{1,0:T(8,128)(2,1)S(1)}, bf16[128,2048]{1,0:T(8,128)(2,1)}, u32[]{:S(2)}, u32[]{:S(2)}) %collective-permute-start.40) | collective-permute-done | bytes 524320 | tf_op jit(solution)/shard_map/ppermute | solution.py:69
  167.1 8.4 collective-permute-done.42
  179.3 7.4 collective-permute-done.5
  190.4 7.6 collective-permute-done.44
  213.4 7.9 fusion.133
  221.5 21.0 %psum.14 = f32[2,1024]{1,0:T(2,128)} all-reduce(f32[2,1024]{1,0:T(2,128)S(1)} %pad_maximum_fusion.17), channel_id=1, replica_groups=mesh['head'=8,'fsdp'=4] {'head'}, use_global_device_ids=true, to_apply=%region_3.4 | all-reduce | flops 2048 | bytes 16384 | tf_op jit(solution)/shard_map/psum | solution.py:189
  259.1 8.8 %collective-permute-done.15 = bf16[1024,256]{0,1:T(8,128)(2,1)S(1)} collective-permute-done((bf16[1024,256]{0,1:T(8,128)(2,1)S(1)}, bf16[1024,256]{0,1:T(8,128)(2,1)S(1)}, u32[]{:S(2)}, u32[]{:S(2)}) %collective-permute-start.15) | collective-permute-done | bytes 524320 | tf_op jit(solution)/shard_map/ppermute | solution.py:68
  300.7 14.3 %multiply_reduce_fusion = (f32[1024]{0:T(1024)S(1)}, f32[1024,2048]{1,0:T(8,128)S(1)}) fusion(bf16[1024,2048]{0,1:T(8,128)(2,1)} %bitcast.54, bf16[2048,2048]{1,0:T(8,128)(2,1)} %all-gather.8.cloned.1.call-done, bf16[8,128,2048]{2,1,0:T(8,128)(2,1)} %fusion.75), kind=kOutput, calls=%fused_computation.31 | convolution fusion | flops 8598322176 | bytes 25169920 | tf_op jit(solution)/shard_map/dot_general | solution.py:115
  327.6 10.1 %fusion.18 = f32[1024,1024]{1,0:T(8,128)} fusion(bf16[1024,2048]{1,0:T(8,128)(2,1)} %copy-done.6, bf16[2,2048,1024]{2,1,0:T(8,128)(2,1)} %all-gather.10.cloned.1.call-done), kind=kOutput, calls=%fused_computation.68 | convolution fusion | flops 4294967296 | bytes 12582912 | tf_op jit(solution)/shard_map/dot_general | solution.py:115
  344.2 10.1 %fusion.20 = f32[1024,1024]{1,0:T(8,128)} fusion(bf16[1024,2048]{1,0:T(8,128)(2,1)} %copy-done.6, bf16[2,2048,1024]{2,1,0:T(8,128)(2,1)} %all-gather.12.cloned.1.call-done), kind=kOutput, calls=%fused_computation.70 | convolution fusion | flops 4294967296 | bytes 12582912 | tf_op jit(solution)/shard_map/dot_general | solution.py:115
  360.5 12.2 %multiply_convert_fusion.5 = (bf16[1024,1024]{1,0:T(8,128)(2,1)S(1)}, bf16[1024,1024]{1,0:T(8,128)(2,1)S(1)}, bf16[1024,1024]{1,0:T(8,128)(2,1)}) fusion(f32[1024,1024]{1,0:T(8,128)} %fusion.18, f32[1024,1024]{1,0:T(8,128)} %fusion.20, bf16[1024,2048]{1,0:T(8,128)(2,1)} %bitcast.485, bf16[2,1024,2048]{2,1,0:T(8,128)(2,1)} %all-gather.14.cloned.1.call-done), kind=kOutput, calls=%fused_computation.50 | convolution fusion | flops 4310695936 | bytes 23068672 | tf_op jit(solution)/shard_map/dot_general | solution.py:115
  372.7 10.4 %fusion.17 = f32[1024,2048]{1,0:T(8,128)} fusion(bf16[1024,1024]{1,0:T(8,128)(2,1)S(1)} %get-tuple-element.89, bf16[2,2048,1024]{2,1,0:T(8,128)(2,1)} %all-gather.10.cloned.1.call-done), kind=kOutput, calls=%fused_computation.67 | convolution fusion | flops 4294967296 | bytes 14680064 | tf_op jit(solution)/shard_map/dot_general | solution.py:115
  383.1 9.1 %fusion.19 = f32[1024,2048]{1,0:T(8,128)} fusion(bf16[1024,1024]{1,0:T(8,128)(2,1)S(1)} %get-tuple-element.88, bf16[2,2048,1024]{2,1,0:T(8,128)(2,1)} %all-gather.12.cloned.1.call-done), kind=kOutput, calls=%fused_computation.69 | convolution fusion | flops 4294967296 | bytes 14680064 | tf_op jit(solution)/shard_map/dot_general | solution.py:115
  392.3 10.4 %multiply_convert_fusion.3 = (bf16[1024,1024]{1,0:T(8,128)(2,1)S(1)}, bf16[1024,1024]{1,0:T(8,128)(2,1)}, bf16[1024,1024]{1,0:T(8,128)(2,1)}) fusion(f32[1024,1024]{1,0:T(8,128)} %fusion.23, f32[1024,1024]{1,0:T(8,128)} %fusion.24, bf16[1024,2048]{1,0:T(8,128)(2,1)S(1)} %bitcast.484, bf16[2,1024,2048]{2,1,0:T(8,128)(2,1)S(1)} %bitcast.562), kind=kOutput, calls=%fused_computation.48 | convolution fusion | flops 4310695936 | bytes 23068672 | tf_op jit(solution)/shard_map/dot_general | solution.py:115
  402.7 9.1 %fusion.22 = f32[1024,2048]{1,0:T(8,128)} fusion(bf16[1024,1024]{1,0:T(8,128)(2,1)} %get-tuple-element.86, bf16[2,2048,1024]{2,1,0:T(8,128)(2,1)S(1)} %bitcast.564), kind=kOutput, calls=%fused_computation.72 | convolution fusion | flops 4294967296 | bytes 14680064 | tf_op jit(solution)/shard_map/dot_general | solution.py:115
  411.9 13.3 %add_convert_fusion = bf16[1024,2048]{1,0:T(8,128)(2,1)} fusion(f32[1024,2048]{1,0:T(8,128)} %fusion.22, f32[1024,2048]{1,0:T(8,128)} %fusion.17, f32[1024,2048]{1,0:T(8,128)} %fusion.19, bf16[1024,1024]{1,0:T(8,128)(2,1)S(1)} %get-tuple-element.85, bf16[2,2048,1024]{2,1,0:T(8,128)(2,1)} %all-gather.12.cloned.1.call-done), kind=kOutput, calls=%fused_computation.29 | convolution fusion | flops 4303355904 | bytes 35651584 | tf_op jit(solution)/shard_map/dot_general | solution.py:115
  439.6 12.6 %collective-permute-done.48 = bf16[128,2048]{1,0:T(8,128)(2,1)S(1)} collective-permute-done((bf16[128,2048]{1,0:T(8,128)(2,1)S(1)}, bf16[128,2048]{1,0:T(8,128)(2,1)S(1)}, u32[]{:S(2)}, u32[]{:S(2)}) %collective-permute-start.48) | collective-permute-done | bytes 524320 | tf_op jit(solution)/shard_map/ppermute | solution.py:98
  453.7 7.5 convolution_convert_fusion.1
  466.0 12.6 %fusion.2 = (f32[1024]{0:T(1024)S(1)}, f32[1024]{0:T(1024)S(1)}, bf16[1024,2048]{1,0:T(8,128)(2,1)}, bf16[1024,2048]{1,0:T(8,128)(2,1)}, bf16[1024,2048]{1,0:T(8,128)(2,1)}) fusion(bf16[8,128,2048]{2,1,0:T(8,128)(2,1)} %fusion.77, bf16[1024,2048]{1,0:T(8,128)(2,1)S(1)} %convolution_convert_fusion.1, f32[1024]{0:T(1024)S(1)} %bitcast.532, ...), kind=kOutput, calls=%fused_computation.7 | convolution fusion | flops 4328519680 | bytes 27279360 | tf_op jit(solution)/shard_map/dot_general | solution.py:115
  543.0 19.8 %psum.15 = f32[2,1024]{1,0:T(2,128)S(1)} all-reduce(f32[2,1024]{1,0:T(2,128)S(1)} %pad_maximum_fusion.18), channel_id=1, replica_groups=mesh['head'=8,'fsdp'=4] {'head'}, use_global_device_ids=true, to_apply=%region_23.24 | all-reduce | flops 2048 | bytes 16384 | tf_op jit(solution)/shard_map/psum | solution.py:303
  570.8 7.7 convert_bitcast_fusion.1
  591.1 7.6 convert_bitcast_fusion.3
  613.2 7.5 convert_bitcast_fusion.5
  647.6 7.8 collective-permute-done.63
  663.7 11.4 %collective-permute-done.65 = bf16[128,2048]{1,0:T(8,128)(2,1)S(1)} collective-permute-done((bf16[128,2048]{1,0:T(8,128)(2,1)S(1)}, bf16[128,2048]{1,0:T(8,128)(2,1)S(1)}, u32[]{:S(2)}, u32[]{:S(2)}) %collective-permute-start.65) | collective-permute-done | bytes 524320 | tf_op jit(solution)/shard_map/ppermute | solution.py:68
  690.0 8.3 collective-permute-done.56
  707.8 10.3 %collective-permute-done.57 = bf16[128,2048]{1,0:T(8,128)(2,1)} collective-permute-done((bf16[128,2048]{1,0:T(8,128)(2,1)S(1)}, bf16[128,2048]{1,0:T(8,128)(2,1)}, u32[]{:S(2)}, u32[]{:S(2)}) %collective-permute-start.57) | collective-permute-done | bytes 524320 | tf_op jit(solution)/shard_map/ppermute | solution.py:98
  762.1 23.5 %collective-permute-done.38 = bf16[128,2048]{1,0:T(8,128)(2,1)S(1)} collective-permute-done((bf16[128,2048]{1,0:T(8,128)(2,1)S(1)}, bf16[128,2048]{1,0:T(8,128)(2,1)S(1)}, u32[]{:S(2)}, u32[]{:S(2)}) %collective-permute-start.38) | collective-permute-done | bytes 524320 | tf_op jit(solution)/shard_map/ppermute | solution.py:99
  803.1 26.6 %reduce-scatter.10.cloned.1.call-done = bf16[2,512,1024]{2,1,0:T(8,128)(2,1)} async-done(((bf16[2,2048,1024]{2,1,0:T(8,128)(2,1)}), bf16[2,512,1024]{2,1,0:T(8,128)(2,1)}) %reduce-scatter.10.cloned.1.call-update) | async-done | bytes 2097168 | tf_op jit(solution)/shard_map/reduce_scatter | solution.py:253
  833.8 30.3 %reduce-scatter.8.cloned.1.call-done = f32[64,2048]{1,0:T(8,128)} async-done(((f32[256,2048]{1,0:T(8,128)}), f32[64,2048]{1,0:T(8,128)}) %reduce-scatter.8.cloned.1.call-update) | async-done | bytes 524304 | tf_op jit(solution)/shard_map/reduce_scatter | solution.py:322
  (551 shorter events, 410.5 us)
Async XLA Ops:
  7.2 206.3 %all-gather.16.cloned.1.call-start = ((), (), s32[]{:S(2)}) async-start(), calls=%async_computation.18 | async-start | bytes 3932160 | tf_op jit(solution)/shard_map/all_gather | solution.py:169
  34.5 266.2 %all-gather.8.cloned.1.call-start = ((), (), s32[]{:S(2)}) async-start(), calls=%async_computation.9 | async-start | bytes 8650752 | tf_op jit(solution)/shard_map/all_gather | solution.py:172
  35.3 292.4 %all-gather.10.cloned.1.call-start = ((), (), s32[]{:S(2)}) async-start(), calls=%async_computation.10 | async-start | bytes 10485760 | tf_op jit(solution)/shard_map/all_gather | solution.py:173
  36.0 308.2 %all-gather.12.cloned.1.call-start = ((), (), s32[]{:S(2)}) async-start(), calls=%async_computation.11 | async-start | bytes 10485760 | tf_op jit(solution)/shard_map/all_gather | solution.py:174
  36.6 323.9 %all-gather.14.cloned.1.call-start = ((), (), s32[]{:S(2)}) async-start(), calls=%async_computation.12 | async-start | bytes 10485760 | tf_op jit(solution)/shard_map/all_gather | solution.py:175
  36.6 73.1 %collective-permute-start.23 = (s32[128,16]{0,1:T(8,128)S(1)}, s32[128,16]{0,1:T(8,128)S(1)}, u32[]{:S(2)}, u32[]{:S(2)}) collective-permute-start(s32[128,16]{0,1:T(8,128)S(1)} %pad_add_fusion), channel_id=1, source_target_pairs={{0,8},{8,16},{16,24},{24,28},{28,20},{20,12},{12,4},{4,0},{1,9},{9... | collective-permute-start | bytes 24584 | tf_op jit(solution)/shard_map/ppermute | solution.py:68
  40.6 69.2 %collective-permute-start.24 = (s32[128,16]{0,1:T(8,128)S(1)}, s32[128,16]{0,1:T(8,128)S(1)}, u32[]{:S(2)}, u32[]{:S(2)}) collective-permute-start(s32[128,16]{0,1:T(8,128)S(1)} %pad_add_fusion), channel_id=1, source_target_pairs={{8,0},{16,8},{24,16},{28,24},{20,28},{12,20},{4,12},{0,4},{9,1},{1... | collective-permute-start | bytes 24584 | tf_op jit(solution)/shard_map/ppermute | solution.py:69
  40.6 82.6 %collective-permute-start = (bf16[128,2048]{1,0:T(8,128)(2,1)S(1)}, bf16[128,2048]{1,0:T(8,128)(2,1)S(1)}, u32[]{:S(2)}, u32[]{:S(2)}) collective-permute-start(bf16[128,2048]{1,0:T(8,128)(2,1)S(1)} %bitcast.451), channel_id=1, source_target_pairs={{0,8},{8,16},{16,24},{24,28},{28,20},{20,12},{12,4},{4,0},{1,9},{9... | collective-permute-start | bytes 1572872 | tf_op jit(solution)/shard_map/ppermute | solution.py:68
  42.7 81.6 %collective-permute-start.1 = (bf16[128,2048]{1,0:T(8,128)(2,1)S(1)}, bf16[128,2048]{1,0:T(8,128)(2,1)S(1)}, u32[]{:S(2)}, u32[]{:S(2)}) collective-permute-start(bf16[128,2048]{1,0:T(8,128)(2,1)S(1)} %bitcast.452), channel_id=1, source_target_pairs={{8,0},{16,8},{24,16},{28,24},{20,28},{12,20},{4,12},{0,4},{9,1},{1... | collective-permute-start | bytes 1572872 | tf_op jit(solution)/shard_map/ppermute | solution.py:69
  42.7 84.3 %collective-permute-start.39 = (bf16[128,2048]{1,0:T(8,128)(2,1)S(1)}, bf16[128,2048]{1,0:T(8,128)(2,1)S(1)}, u32[]{:S(2)}, u32[]{:S(2)}) collective-permute-start(bf16[128,2048]{1,0:T(8,128)(2,1)S(1)} %bitcast.465), channel_id=1, source_target_pairs={{0,8},{8,16},{16,24},{24,28},{28,20},{20,12},{12,4},{4,0},{1,9},{9... | collective-permute-start | bytes 1572872 | tf_op jit(solution)/shard_map/ppermute | solution.py:68
  121.2 31.6 %collective-permute-start.40 = (bf16[128,2048]{1,0:T(8,128)(2,1)S(1)}, bf16[128,2048]{1,0:T(8,128)(2,1)}, u32[]{:S(2)}, u32[]{:S(2)}) collective-permute-start(bf16[128,2048]{1,0:T(8,128)(2,1)S(1)} %bitcast.466), channel_id=1, source_target_pairs={{8,0},{16,8},{24,16},{28,24},{20,28},{12,20},{4,12},{0,4},{9,1},{1... | collective-permute-start | bytes 1572872 | tf_op jit(solution)/shard_map/ppermute | solution.py:69
  123.3 31.5 %collective-permute-start.2 = (bf16[128,2048]{1,0:T(8,128)(2,1)S(1)}, bf16[128,2048]{1,0:T(8,128)(2,1)S(1)}, u32[]{:S(2)}, u32[]{:S(2)}) collective-permute-start(bf16[128,2048]{1,0:T(8,128)(2,1)S(1)} %collective-permute-done), channel_id=1, source_target_pairs={{0,8},{8,16},{16,24},{24,28},{28,20},{20,12},{12,4},{4,0},{1,9},{9... | collective-permute-start | bytes 1572872 | tf_op jit(solution)/shard_map/ppermute | solution.py:68
  124.3 40.0 %collective-permute-start.3 = (bf16[128,2048]{1,0:T(8,128)(2,1)S(1)}, bf16[128,2048]{1,0:T(8,128)(2,1)S(1)}, u32[]{:S(2)}, u32[]{:S(2)}) collective-permute-start(bf16[128,2048]{1,0:T(8,128)(2,1)S(1)} %collective-permute-done.1), channel_id=1, source_target_pairs={{8,0},{16,8},{24,16},{28,24},{20,28},{12,20},{4,12},{0,4},{9,1},{1... | collective-permute-start | bytes 1572872 | tf_op jit(solution)/shard_map/ppermute | solution.py:69
  127.0 37.3 %collective-permute-start.41 = (bf16[128,2048]{1,0:T(8,128)(2,1)S(1)}, bf16[128,2048]{1,0:T(8,128)(2,1)S(1)}, u32[]{:S(2)}, u32[]{:S(2)}) collective-permute-start(bf16[128,2048]{1,0:T(8,128)(2,1)S(1)} %collective-permute-done.39), channel_id=1, source_target_pairs={{0,8},{8,16},{16,24},{24,28},{28,20},{20,12},{12,4},{4,0},{1,9},{9... | collective-permute-start | bytes 1572872 | tf_op jit(solution)/shard_map/ppermute | solution.py:68
  152.8 22.7 %collective-permute-start.42 = (bf16[128,2048]{1,0:T(8,128)(2,1)}, bf16[128,2048]{1,0:T(8,128)(2,1)S(1)}, u32[]{:S(2)}, u32[]{:S(2)}) collective-permute-start(bf16[128,2048]{1,0:T(8,128)(2,1)} %collective-permute-done.40), channel_id=1, source_target_pairs={{8,0},{16,8},{24,16},{28,24},{20,28},{12,20},{4,12},{0,4},{9,1},{1... | collective-permute-start | bytes 1572872 | tf_op jit(solution)/shard_map/ppermute | solution.py:69
  154.8 22.5 %collective-permute-start.4 = (bf16[128,2048]{1,0:T(8,128)(2,1)S(1)}, bf16[128,2048]{1,0:T(8,128)(2,1)S(1)}, u32[]{:S(2)}, u32[]{:S(2)}) collective-permute-start(bf16[128,2048]{1,0:T(8,128)(2,1)S(1)} %collective-permute-done.2), channel_id=1, source_target_pairs={{0,8},{8,16},{16,24},{24,28},{28,20},{20,12},{12,4},{4,0},{1,9},{9... | collective-permute-start | bytes 1572872 | tf_op jit(solution)/shard_map/ppermute | solution.py:68
  164.3 22.6 %collective-permute-start.43 = (bf16[128,2048]{1,0:T(8,128)(2,1)S(1)}, bf16[128,2048]{1,0:T(8,128)(2,1)S(1)}, u32[]{:S(2)}, u32[]{:S(2)}) collective-permute-start(bf16[128,2048]{1,0:T(8,128)(2,1)S(1)} %collective-permute-done.41), channel_id=1, source_target_pairs={{0,8},{8,16},{16,24},{24,28},{28,20},{20,12},{12,4},{4,0},{1,9},{9... | collective-permute-start | bytes 1572872 | tf_op jit(solution)/shard_map/ppermute | solution.py:68
  177.3 24.3 %collective-permute-start.6 = (bf16[64,2048]{1,0:T(8,128)(2,1)S(1)}, bf16[64,2048]{1,0:T(8,128)(2,1)S(1)}, u32[]{:S(2)}, u32[]{:S(2)}) collective-permute-start(bf16[64,2048]{1,0:T(8,128)(2,1)S(1)} %slice.412), channel_id=1, source_target_pairs={{0,8},{8,16},{16,24},{24,28},{28,20},{20,12},{12,4},{4,0},{1,9},{9... | collective-permute-start | bytes 786440 | tf_op jit(solution)/shard_map/ppermute | solution.py:72
  188.4 81.9 %collective-permute-start.45 = (bf16[64,2048]{1,0:T(8,128)(2,1)}, bf16[64,2048]{1,0:T(8,128)(2,1)}, u32[]{:S(2)}, u32[]{:S(2)}) collective-permute-start(bf16[64,2048]{1,0:T(8,128)(2,1)} %slice.445), channel_id=1, source_target_pairs={{0,8},{8,16},{16,24},{24,28},{28,20},{20,12},{12,4},{4,0},{1,9},{9... | collective-permute-start | bytes 786440 | tf_op jit(solution)/shard_map/ppermute | solution.py:72
  199.5 70.8 %collective-permute-start.46 = (bf16[64,2048]{1,0:T(8,128)(2,1)}, bf16[64,2048]{1,0:T(8,128)(2,1)}, u32[]{:S(2)}, u32[]{:S(2)}) collective-permute-start(bf16[64,2048]{1,0:T(8,128)(2,1)} %slice.446), channel_id=1, source_target_pairs={{8,0},{16,8},{24,16},{28,24},{20,28},{12,20},{4,12},{0,4},{9,1},{1... | collective-permute-start | bytes 786440 | tf_op jit(solution)/shard_map/ppermute | solution.py:73
  438.3 22.8 %collective-permute-start.52 = (bf16[128,2048]{1,0:T(8,128)(2,1)S(1)}, bf16[128,2048]{1,0:T(8,128)(2,1)S(1)}, u32[]{:S(2)}, u32[]{:S(2)}) collective-permute-start(bf16[128,2048]{1,0:T(8,128)(2,1)S(1)} %pad_maximum_fusion.12), channel_id=1, source_target_pairs={{8,0},{16,8},{24,16},{28,24},{20,28},{12,20},{4,12},{0,4},{9,1},{1... | collective-permute-start | bytes 1572872 | tf_op jit(solution)/shard_map/ppermute | solution.py:99
  514.6 240.0 %reduce-scatter.6.cloned.1.call-start = ((), (), s32[]{:S(2)}) async-start(), calls=%async_computation.13 | async-start | bytes 3932160 | tf_op jit(solution)/shard_map/reduce_scatter | solution.py:317
  570.6 224.3 %reduce-scatter.14.cloned.1.call-start = ((), (), s32[]{:S(2)}) async-start(), calls=%async_computation.17 | async-start | bytes 10485760 | tf_op jit(solution)/shard_map/reduce_scatter | solution.py:253
  591.1 208.0 %reduce-scatter.12.cloned.1.call-start = ((), (), s32[]{:S(2)}) async-start(), calls=%async_computation.16 | async-start | bytes 10485760 | tf_op jit(solution)/shard_map/reduce_scatter | solution.py:253
  611.4 218.3 %reduce-scatter.10.cloned.1.call-start = ((), (), s32[]{:S(2)}) async-start(), calls=%async_computation.15 | async-start | bytes 10485760 | tf_op jit(solution)/shard_map/reduce_scatter | solution.py:253
  633.4 230.8 %reduce-scatter.8.cloned.1.call-start = ((), (), s32[]{:S(2)}) async-start(), calls=%async_computation.14 | async-start | bytes 2621440 | tf_op jit(solution)/shard_map/reduce_scatter | solution.py:322
  645.4 85.0 %collective-permute-start.36 = (bf16[128,2048]{1,0:T(8,128)(2,1)S(1)}, bf16[128,2048]{1,0:T(8,128)(2,1)}, u32[]{:S(2)}, u32[]{:S(2)}) collective-permute-start(bf16[128,2048]{1,0:T(8,128)(2,1)S(1)} %pad_maximum_fusion.10), channel_id=1, source_target_pairs={{8,0},{16,8},{24,16},{28,24},{20,28},{12,20},{4,12},{0,4},{9,1},{1... | collective-permute-start | bytes 1572872 | tf_op jit(solution)/shard_map/ppermute | solution.py:99
  646.7 73.4 %collective-permute-start.32 = (bf16[128,2048]{1,0:T(8,128)(2,1)S(1)}, bf16[128,2048]{1,0:T(8,128)(2,1)S(1)}, u32[]{:S(2)}, u32[]{:S(2)}) collective-permute-start(bf16[128,2048]{1,0:T(8,128)(2,1)S(1)} %pad_maximum_fusion.9), channel_id=1, source_target_pairs={{0,8},{8,16},{16,24},{24,28},{28,20},{20,12},{12,4},{4,0},{1,9},{9... | collective-permute-start | bytes 1572872 | tf_op jit(solution)/shard_map/ppermute | solution.py:98
  682.6 25.2 %collective-permute-start.60 = (bf16[128,2048]{1,0:T(8,128)(2,1)S(1)}, bf16[128,2048]{1,0:T(8,128)(2,1)}, u32[]{:S(2)}, u32[]{:S(2)}) collective-permute-start(bf16[128,2048]{1,0:T(8,128)(2,1)S(1)} %pad_maximum_fusion.14), channel_id=1, source_target_pairs={{8,0},{16,8},{24,16},{28,24},{20,28},{12,20},{4,12},{0,4},{9,1},{1... | collective-permute-start | bytes 1572872 | tf_op jit(solution)/shard_map/ppermute | solution.py:99
  733.6 24.7 %collective-permute-start.37 = (bf16[128,2048]{1,0:T(8,128)(2,1)}, bf16[128,2048]{1,0:T(8,128)(2,1)}, u32[]{:S(2)}, u32[]{:S(2)}) collective-permute-start(bf16[128,2048]{1,0:T(8,128)(2,1)} %get-tuple-element.113), channel_id=1, source_target_pairs={{8,0},{16,8},{24,16},{28,24},{20,28},{12,20},{4,12},{0,4},{9,1},{1... | collective-permute-start | bytes 1572872 | tf_op jit(solution)/shard_map/ppermute | solution.py:99
  754.6 36.8 %all-to-all-start.2 = ((bf16[8,64,768]{2,1,0:T(8,128)(2,1)}), bf16[8,64,768]{2,1,0:T(8,128)(2,1)S(1)}, u32[]{:S(2)}, u32[]{:S(2)}) async-start(bf16[8,64,768]{2,1,0:T(8,128)(2,1)} %reduce-scatter.6.cloned.1.call-done), calls=%async_computation.3 | async-start | bytes 1572864 | tf_op jit(solution)/shard_map/all_to_all | solution.py:318
  759.5 26.1 %collective-permute-start.38 = (bf16[128,2048]{1,0:T(8,128)(2,1)S(1)}, bf16[128,2048]{1,0:T(8,128)(2,1)S(1)}, u32[]{:S(2)}, u32[]{:S(2)}) collective-permute-start(bf16[128,2048]{1,0:T(8,128)(2,1)S(1)} %fusion.60), channel_id=1, source_target_pairs={{8,0},{16,8},{24,16},{28,24},{20,28},{12,20},{4,12},{0,4},{9,1},{1... | collective-permute-start | bytes 1572872 | tf_op jit(solution)/shard_map/ppermute | solution.py:99
  (148 other events, 1954.9 us)
Sparse Core Ops, SparseCore 0:
  34.6 30.8 all-gather.15
  68.4 90.9 all-gather.7
  161.0 65.7 all-gather.9
  228.2 58.2 all-gather.11
  287.9 58.2 all-gather.13
  570.7 33.8 reduce-scatter.5
  607.4 71.7 reduce-scatter.13
  681.7 73.3 reduce-scatter.11
  757.9 71.7 reduce-scatter.9
  832.7 31.4 reduce-scatter.7
